TPU v7x, 32 devices: a whole 2x2x4 slice. The times are simulated.
32 devices in a mesh: wide: 8 (over y, x, core), blk: 4 (over z).
Axes of the slice: x: 2, y: 2, z: 4, core: 2. Of those that a mesh axis runs over, the one named last changes fastest.
Arguments:
- left_points: float32 [4096], P(('wide', 'blk')), may hold values from -1 to 1, as said below
- left_ports: int32 [4096], P(('wide', 'blk')), may hold values from 0 to 63
- left_values: bfloat16 [4096, 64], P(('wide', 'blk')), may hold values from -6 to 6
- right_points: float32 [2048], P('blk'), may hold values from -1 to 1
- right_ports: int32 [2048], P('blk'), may hold values from 0 to 63
- right_values: bfloat16 [2048, 64], P('blk'), may hold values from -6 to 6
- sketch_block: int32 [2048], P('blk'), may hold values from 0 to 63, as said below
- sketch_weight: bfloat16 [2048], P('blk'), may hold values from -1 to 1
Outputs:
- basis: float32 [4096, 64], P(('wide', 'blk'))
- projected: float32 [64, 64], replicated
Inputs may be any that keep to these rules, and one draw needn't show every extreme that they name: `left_points`: no left point lies closer than 0.6 / 2048 to any right point. `sketch_block`: in every aligned run of 64 right samples each sketch column appears exactly once.
All inputs are finite; a program needn't handle non-finite values.
Results may differ from a plain program's by a relative error of at most 0.0019.
Values sent between devices are 32-bit elements; how exact they have to be, the bound alone decides.
No kernel may reach another device: no remote copies, remote signals or barrier semaphores. Data moves between devices by JAX's collectives and lax.ppermute only.
A program may use at most 64 MiB of HBM per device.

v0:
```python
import jax
import jax.numpy as jnp
from jax import lax
from jax.sharding import PartitionSpec as P

K = 64


def cholesky_lower(gram):
    order = gram.shape[0]
    index_ids = jnp.arange(order, dtype=jnp.int32)

    def column_step(j, lower):
        row_j = lax.dynamic_slice_in_dim(lower, j, 1, 0)[0]
        column = lax.dynamic_slice_in_dim(gram, j, 1, 1)[:, 0] - jnp.dot(
            lower, row_j, precision=lax.Precision.HIGHEST
        )
        pivot = jnp.sqrt(lax.dynamic_slice_in_dim(column, j, 1, 0)[0])
        fresh = jnp.where(
            index_ids > j,
            column / pivot,
            jnp.where(index_ids == j, pivot, jnp.zeros((), gram.dtype)),
        )
        marker = (index_ids == j).astype(gram.dtype)
        return lower + fresh[:, None] * marker[None, :]

    return lax.fori_loop(0, order, column_step, jnp.zeros_like(gram))


def solve_lower(lower, rhs):
    order = lower.shape[0]
    index_ids = jnp.arange(order, dtype=jnp.int32)

    def row_step(j, result):
        row_j = lax.dynamic_slice_in_dim(lower, j, 1, 0)[0]
        pivot = lax.dynamic_slice_in_dim(row_j, j, 1, 0)[0]
        target = lax.dynamic_slice_in_dim(rhs, j, 1, 0)[0]
        value = (target - jnp.dot(row_j, result, precision=lax.Precision.HIGHEST)) / pivot
        marker = (index_ids == j).astype(rhs.dtype)
        return result + marker[:, None] * value[None, :]

    return lax.fori_loop(0, order, row_step, jnp.zeros_like(rhs))


def solve_upper(upper, rhs):
    order = upper.shape[0]
    index_ids = jnp.arange(order, dtype=jnp.int32)

    def row_step(step, result):
        j = order - 1 - step
        row_j = lax.dynamic_slice_in_dim(upper, j, 1, 0)[0]
        pivot = lax.dynamic_slice_in_dim(row_j, j, 1, 0)[0]
        target = lax.dynamic_slice_in_dim(rhs, j, 1, 0)[0]
        value = (target - jnp.dot(row_j, result, precision=lax.Precision.HIGHEST)) / pivot
        marker = (index_ids == j).astype(rhs.dtype)
        return result + marker[:, None] * value[None, :]

    return lax.fori_loop(0, order, row_step, jnp.zeros_like(rhs))


def tile_sketch(left_freq, left_onehot, left_values, points, ports, values_block, columns, weights):
    amount = points.shape[0]
    block_count = amount // amount
    port_ids = jnp.arange(left_values.shape[1], dtype=jnp.int32)
    column_ids = jnp.arange(K, dtype=jnp.int32)

    def absorb(carry, items):
        freq, port_block, value_rows, column_block, weight_block = items
        onehot_right = (port_ids[:, None] == port_block[None, :]).astype(jnp.float32)
        num_v = jnp.dot(
            left_values,
            onehot_right,
            precision=lax.Precision.HIGHEST,
            preferred_element_type=jnp.float32,
        )
        num_w = lax.dot_general(
            left_onehot,
            value_rows,
            (((1,), (1,)), ((), ())),
            precision=lax.Precision.HIGHEST,
            preferred_element_type=jnp.float32,
        )
        inverse = 1.0 / (left_freq[:, None] - freq[None, :])
        loewner = (num_v - num_w) * inverse
        shifted = (left_freq[:, None] * num_v - freq[None, :] * num_w) * inverse
        omega = jnp.where(
            column_block[:, None] == column_ids[None, :],
            weight_block[:, None],
            jnp.zeros((), jnp.float32),
        )
        sketch_part = jnp.dot(
            loewner, omega, precision=lax.Precision.HIGHEST, preferred_element_type=jnp.float32
        )
        shift_part = jnp.dot(
            shifted, omega, precision=lax.Precision.HIGHEST, preferred_element_type=jnp.float32
        )
        return ((carry[0] + sketch_part, carry[1] + shift_part), None)

    row_count = left_values.shape[0]
    start_carry = (jnp.zeros((row_count, K), jnp.float32), jnp.zeros((row_count, K), jnp.float32))
    items = (
        points.reshape(block_count, amount),
        ports.reshape(block_count, amount),
        values_block.reshape(block_count, amount, values_block.shape[1]),
        columns.reshape(block_count, amount),
        weights.reshape(block_count, amount),
    )
    result, _ = lax.scan(absorb, start_carry, items)
    return result


def left_setup(points, ports, width):
    port_ids = jnp.arange(width, dtype=jnp.int32)
    onehot_left = (ports[:, None] == port_ids[None, :]).astype(jnp.float32)
    return (points, onehot_left)


def per_device(
    left_points,
    left_ports,
    left_values,
    right_points,
    right_ports,
    right_values,
    sketch_block,
    sketch_weight,
):
    row_count = left_points.shape[0]
    width = left_values.shape[1]
    left_wide = left_values.astype(jnp.float32)
    group_points, group_ports, group_values = (
        lax.all_gather(left_points, "blk", axis=0, tiled=True),
        lax.all_gather(left_ports, "blk", axis=0, tiled=True),
        lax.all_gather(left_wide, "blk", axis=0, tiled=True),
    )
    right_wide = right_values.astype(jnp.float32)
    weight_wide = sketch_weight.astype(jnp.float32)
    left_freq, left_onehot = left_setup(group_points, group_ports, width)
    sketch_part, shift_part = tile_sketch(
        left_freq,
        left_onehot,
        group_values,
        right_points,
        right_ports,
        right_wide,
        sketch_block,
        weight_wide,
    )
    stacked = lax.psum_scatter(
        jnp.concatenate([sketch_part, shift_part], axis=1), "blk", scatter_dimension=0, tiled=True
    )
    sketch = stacked[:, :K]
    shifted_sketch = stacked[:, K:]
    row_total = row_count * lax.axis_size("wide") * lax.axis_size("blk")
    gram_local = jnp.dot(sketch.T, sketch, precision=lax.Precision.HIGHEST)
    gram = lax.psum(gram_local, ("wide", "blk")) / row_total
    lower = cholesky_lower(gram)
    basis_t = solve_lower(lower, sketch.T)
    projection_local = jnp.dot(basis_t, shifted_sketch, precision=lax.Precision.HIGHEST)
    coefficient = lax.psum(projection_local, ("wide", "blk")) / row_total
    projected = solve_upper(lower.T, coefficient)
    return (basis_t.T, projected)


def solution(mesh):
    placed = (
        P(("wide", "blk")),
        P(("wide", "blk")),
        P(("wide", "blk"), None),
        P("blk"),
        P("blk"),
        P("blk", None),
        P("blk"),
        P("blk"),
    )
    return jax.shard_map(
        per_device,
        mesh=mesh,
        in_specs=placed,
        out_specs=(P(("wide", "blk"), None), P()),
        check_vma=False,
    )
```

profile of v0, /device:TPU:0, one launch (start us, length us, event | category | flops | bytes accessed | tf_op | source)
XLA Modules:
  0.0 438.6 jit_solution(5190188491721261414)
XLA Ops:
  7.9 15.1 %all_gather.9 = f32[512,64]{0,1:T(8,128)S(1)} all-gather(f32[128,64]{0,1:T(8,128)S(1)} %convert_element_type.55), channel_id=1, replica_groups=mesh['wide'=8,'blk'=4] {'blk'}, dimensions={0}, use_global_device_ids=true | all-gather | bytes 163840 | tf_op jit(solution)/shard_map/all_gather | solution.py:134
  23.7 11.2 %all-gather = s32[4,1,128]{2,1,0:T(1,128)S(1)} all-gather(s32[1,1,128]{2,1,0:T(1,128)S(1)} %bitcast.82), channel_id=1, replica_groups=mesh['wide'=8,'blk'=4] {'blk'}, dimensions={0}, use_global_device_ids=true | all-gather | bytes 2560 | tf_op jit(solution)/shard_map/all_gather | solution.py:133
  35.6 7.7 %all-gather.1 = f32[4,1,128]{2,1,0:T(1,128)S(1)} all-gather(f32[1,1,128]{2,1,0:T(1,128)S(1)} %bitcast.83), channel_id=1, replica_groups=mesh['wide'=8,'blk'=4] {'blk'}, dimensions={0}, use_global_device_ids=true | all-gather | bytes 2560 | tf_op jit(solution)/shard_map/all_gather | solution.py:132
  45.3 1.1 fusion.28
  46.4 1.0 fusion.33
  48.1 19.8 %reduce-scatter.2.cloned.1.call-done = f32[128,128]{0,1:T(8,128)} async-done(((f32[512,128]{0,1:T(8,128)}), f32[128,128]{0,1:T(8,128)}) %reduce-scatter.2.cloned.1.call-update) | async-done | bytes 65552 | tf_op jit(solution)/shard_map/reduce_scatter | solution.py:149
  67.9 1.0 fusion.55
  68.9 38.6 %psum.14 = f32[64,64]{1,0:T(8,128)S(1)} all-reduce(f32[64,64]{1,0:T(8,128)S(1)} %fusion.55), channel_id=1, replica_groups=mesh['wide'=8,'blk'=4] {'wide','blk'}, use_global_device_ids=true, to_apply=%region_1.2 | all-reduce | flops 4096 | bytes 32768 | tf_op jit(solution)/shard_map/psum | solution.py:156
  107.7 94.5 %while.57 = (s32[]{:T(128)}, f32[64,64]{1,0:T(8,128)S(1)}, f32[64,64]{0,1:T(8,128)S(1)}, s32[]{:T(128)}, s32[]{:T(128)}) while((s32[]{:T(128)}, f32[64,64]{1,0:T(8,128)S(1)}, f32[64,64]{0,1:T(8,128)S(1)}, s32[]{:T(128)}, s32[]{:T(128)}) %tuple.124), condition=%wide.region_3.4_spmd.clone.clone, body=%wide.region_2.3_spmd.clone.clone.sunk | while | flops 66051 | bytes 101992 | solution.py:27
  202.2 93.7 %while.55 = (s32[]{:T(128)}, f32[64,128]{1,0:T(8,128)S(1)}, f32[64,128]{1,0:T(8,128)S(1)}, f32[64,64]{1,0:T(8,128)S(1)}, s32[]{:T(128)}, /*index=5*/s32[]{:T(128)}, s32[]{:T(128)}) while((s32[]{:T(128)}, f32[64,128]{1,0:T(8,128)S(1)}, f32[64,128]{1,0:T(8,128)S(1)}, f32[64,64]{1,0:T(8,128)S(1)}, s32[]{:T(128)}, ...), condition=%wide.region_5.6_spmd.clone, body=%wide.region_4.5_spmd.clone.sunk | while | flops 131460 | bytes 102520 | solution.py:42
  202.8 0.8 fusion.76
  204.3 0.8 fusion.76
  205.7 0.8 fusion.76
  207.2 0.8 fusion.76
  208.7 0.8 fusion.76
  210.1 0.8 fusion.76
  211.6 0.8 fusion.76
  213.1 0.8 fusion.76
  214.5 0.8 fusion.76
  216.0 0.8 fusion.76
  217.5 0.8 fusion.76
  218.9 0.8 fusion.76
  220.4 0.8 fusion.76
  221.8 0.8 fusion.76
  223.3 0.8 fusion.76
  224.8 0.8 fusion.76
  226.2 0.8 fusion.76
  227.7 0.8 fusion.76
  229.2 0.8 fusion.76
  230.6 0.8 fusion.76
  232.1 0.8 fusion.76
  233.6 0.8 fusion.76
  235.0 0.8 fusion.76
  236.5 0.8 fusion.76
  238.0 0.8 fusion.76
  239.4 0.8 fusion.76
  240.9 0.8 fusion.76
  242.3 0.8 fusion.76
  243.8 0.8 fusion.76
  245.3 0.8 fusion.76
  246.7 0.8 fusion.76
  248.2 0.8 fusion.76
  249.7 0.8 fusion.76
  251.1 0.8 fusion.76
  254.1 0.8 fusion.76
  273.1 0.8 fusion.76
  276.0 0.8 fusion.76
  279.0 0.8 fusion.76
  281.9 0.8 fusion.76
  296.6 40.8 %psum.15 = f32[64,64]{1,0:T(8,128)S(1)} all-reduce(f32[64,64]{1,0:T(8,128)S(1)} %fusion.53), channel_id=1, replica_groups=mesh['wide'=8,'blk'=4] {'wide','blk'}, use_global_device_ids=true, to_apply=%region_6.7 | all-reduce | flops 4096 | bytes 32768 | tf_op jit(solution)/shard_map/psum | solution.py:160
  337.5 93.7 %while.56 = (s32[]{:T(128)}, f32[64,64]{1,0:T(8,128)S(1)}, f32[64,64]{1,0:T(8,128)S(1)}, f32[64,64]{1,0:T(8,128)S(1)}, s32[]{:T(128)}, /*index=5*/s32[]{:T(128)}, s32[]{:T(128)}, s32[]{:T(128)}) while((s32[]{:T(128)}, f32[64,64]{1,0:T(8,128)S(1)}, f32[64,64]{1,0:T(8,128)S(1)}, f32[64,64]{1,0:T(8,128)S(1)}, s32[]{:T(128)}, ...), condition=%wide.region_8.9_spmd.clone, body=%wide.region_7.8_spmd.clone.sunk | while | flops 65800 | bytes 69297 | solution.py:58
  342.5 0.8 fusion.79
  348.3 0.8 fusion.79
  355.6 0.8 fusion.79
  363.0 0.8 fusion.79
  370.3 0.8 fusion.79
  376.1 0.8 fusion.79
  383.5 0.8 fusion.79
  390.8 0.8 fusion.79
  398.1 0.8 fusion.79
  403.9 0.8 fusion.79
  411.3 0.8 fusion.79
  418.6 0.8 fusion.79
  425.9 0.8 fusion.79
  (880 shorter events, 207.0 us)
Async XLA Ops:
  7.2 37.4 %copy-start = (bf16[512,64]{0,1:T(8,128)(2,1)S(1)}, bf16[512,64]{0,1:T(8,128)(2,1)}, u32[]{:S(2)}) copy-start(bf16[512,64]{0,1:T(8,128)(2,1)} %param.19) | copy-start | bytes 196612
  7.2 60.7 %reduce-scatter.2.cloned.1.call-start = ((), (), s32[]{:S(2)}) async-start(), calls=%async_computation.1 | async-start | bytes 327680 | tf_op jit(solution)/shard_map/reduce_scatter | solution.py:149
  23.0 0.7 copy-start.6
  34.9 0.7 copy-start.7
  35.6 7.7 %copy-start.5 = (bf16[512]{0:T(512)(128)(2,1)S(1)}, bf16[512]{0:T(512)(128)(2,1)}, u32[]{:S(2)}) copy-start(bf16[512]{0:T(512)(128)(2,1)} %param.21) | copy-start | bytes 3076
  43.3 0.7 copy-start.4
  44.6 0.7 copy-start.8
  44.6 0.7 copy-start.9
  107.7 94.5 %copy-start.3 = (f32[128,128]{0,1:T(8,128)S(1)}, f32[128,128]{0,1:T(8,128)}, u32[]{:S(2)}) copy-start(f32[128,128]{0,1:T(8,128)} %reduce-scatter.2.cloned.1.call-done) | copy-start | bytes 196612
  295.9 0.6 copy-start.1
  431.2 0.6 copy-start.2
Sparse Core Ops, SparseCore 0:
  48.2 19.6 reduce-scatter.1
where the time goes:
time: 441 us; the launch traced here: 439 us
  local copies, waits for them, and re-layouts  119 us (27%)
  matrix products  114 us (26%)
  blocking collectives  113 us (26%)
  loops' own time  40.3 us (9%)
  waiting for transfers between devices  19.8 us (4%)
  other arithmetic  18.2 us (4%)
  between operations  14.2 us (3%)
    dot_general x128, matrix products, row_step(): jnp.dot(row_j, result, precision=lax.Precision.HIGHEST)  100 us
    dynamic_slice x128, local copies, waits for them, and re-layouts, row_step(): pivot = lax.dynamic_slice_in_dim(row_j, j, 1, 0)[0]  76.2 us
    psum x1, blocking collectives, per_device(): coefficient = lax.psum(projection_local, ('wide', 'blk')) / row_total  40.8 us
    another operation x1, loops' own time, cholesky_lower(): return lax.fori_loop(0, order, column_step, jnp.zeros_like(gram))  40 us
    dynamic_slice x64, local copies, waits for them, and re-layouts, column_step(): pivot = jnp.sqrt(lax.dynamic_slice_in_dim(column, j, 1, 0)[0])  39.2 us
    psum x1, blocking collectives, per_device(): gram = lax.psum(gram_local, ('wide', 'blk')) / row_total  38.6 us
    reduce_scatter x1, waiting for transfers between devices, per_device(): lax.psum_scatter(jnp.concatenate([sketch_part, shift_part], axis=1), 'blk...  19.8 us
    all_gather x1, blocking collectives, per_device(): lax.all_gather(left_wide, 'blk', axis=0, tiled=True)  15.1 us
  transfers between devices with their start and end apart: 1, of which 1 were waited for; matrix products, arithmetic and copies ran while one was open for 0% of the time, Pallas kernels for 0%

commit v1 on v0

--- a/solution.py
+++ b/solution.py
@@ -4,6 +4,11 @@
 from jax.sharding import PartitionSpec as P
 
 K = 64
+
+
+def by_each_axis(x, one, other):
+    partial = lax.psum(x, one)
+    return lax.psum(partial, other)
 
 
 def cholesky_lower(gram):
@@ -157,7 +162,7 @@
     lower = cholesky_lower(gram)
     basis_t = solve_lower(lower, sketch.T)
     projection_local = jnp.dot(basis_t, shifted_sketch, precision=lax.Precision.HIGHEST)
-    coefficient = lax.psum(projection_local, ("wide", "blk")) / row_total
+    coefficient = by_each_axis(projection_local, "wide", "blk") / row_total
     projected = solve_upper(lower.T, coefficient)
     return (basis_t.T, projected)
 

time: 441 us -> 446 us (1.011)
    psum x1 -> x2, blocking collectives: 40.8 us -> 41.1 us  [the longest x1 23.1 us: by_each_axis(): partial = lax.psum(x, one)]
where the time goes in v1:
time: 446 us; the launch traced here: 444 us
  local copies, waits for them, and re-layouts  120 us (27%)
  blocking collectives  114 us (26%)
  matrix products  114 us (26%)
  loops' own time  44.1 us (10%)
  waiting for transfers between devices  19.8 us (4%)
  other arithmetic  18.2 us (4%)
  between operations  14.2 us (3%)
    dot_general x128, matrix products, row_step(): jnp.dot(row_j, result, precision=lax.Precision.HIGHEST)  100 us
    dynamic_slice x128, local copies, waits for them, and re-layouts, row_step(): pivot = lax.dynamic_slice_in_dim(row_j, j, 1, 0)[0]  76.2 us
    another operation x1, loops' own time, cholesky_lower(): return lax.fori_loop(0, order, column_step, jnp.zeros_like(gram))  43.8 us
    dynamic_slice x64, local copies, waits for them, and re-layouts, column_step(): pivot = jnp.sqrt(lax.dynamic_slice_in_dim(column, j, 1, 0)[0])  40.2 us
    psum x1, blocking collectives, per_device(): gram = lax.psum(gram_local, ('wide', 'blk')) / row_total  38.6 us
    psum x1, blocking collectives, by_each_axis(): partial = lax.psum(x, one)  23.1 us
    reduce_scatter x1, waiting for transfers between devices, per_device(): lax.psum_scatter(jnp.concatenate([sketch_part, shift_part], axis=1), 'blk...  19.8 us
    psum x1, blocking collectives, by_each_axis(): return lax.psum(partial, other)  17.9 us
  transfers between devices with their start and end apart: 1, of which 1 were waited for; matrix products, arithmetic and copies ran while one was open for 0% of the time, Pallas kernels for 0%

profile of v1, /device:TPU:0, one launch (start us, length us, event | category | flops | bytes accessed | tf_op | source)
XLA Modules:
  0.0 443.6 jit_solution(6099787579286923594)
XLA Ops:
  7.9 15.1 %all_gather.9 = f32[512,64]{0,1:T(8,128)S(1)} all-gather(f32[128,64]{0,1:T(8,128)S(1)} %convert_element_type.55), channel_id=1, replica_groups=mesh['wide'=8,'blk'=4] {'blk'}, dimensions={0}, use_global_device_ids=true | all-gather | bytes 163840 | tf_op jit(solution)/shard_map/all_gather | solution.py:139
  23.7 11.2 %all-gather = s32[4,1,128]{2,1,0:T(1,128)S(1)} all-gather(s32[1,1,128]{2,1,0:T(1,128)S(1)} %bitcast.82), channel_id=1, replica_groups=mesh['wide'=8,'blk'=4] {'blk'}, dimensions={0}, use_global_device_ids=true | all-gather | bytes 2560 | tf_op jit(solution)/shard_map/all_gather | solution.py:138
  35.6 7.7 %all-gather.1 = f32[4,1,128]{2,1,0:T(1,128)S(1)} all-gather(f32[1,1,128]{2,1,0:T(1,128)S(1)} %bitcast.83), channel_id=1, replica_groups=mesh['wide'=8,'blk'=4] {'blk'}, dimensions={0}, use_global_device_ids=true | all-gather | bytes 2560 | tf_op jit(solution)/shard_map/all_gather | solution.py:137
  45.3 1.1 fusion.28
  46.4 1.0 fusion.33
  48.1 19.8 %reduce-scatter.2.cloned.1.call-done = f32[128,128]{0,1:T(8,128)} async-done(((f32[512,128]{0,1:T(8,128)}), f32[128,128]{0,1:T(8,128)}) %reduce-scatter.2.cloned.1.call-update) | async-done | bytes 65552 | tf_op jit(solution)/shard_map/reduce_scatter | solution.py:154
  67.9 1.0 fusion.55
  68.9 38.6 %psum.21 = f32[64,64]{1,0:T(8,128)S(1)} all-reduce(f32[64,64]{1,0:T(8,128)S(1)} %fusion.55), channel_id=1, replica_groups=mesh['wide'=8,'blk'=4] {'wide','blk'}, use_global_device_ids=true, to_apply=%region_1.2 | all-reduce | flops 4096 | bytes 32768 | tf_op jit(solution)/shard_map/psum | solution.py:161
  107.7 99.3 %while.57 = (s32[]{:T(128)}, f32[64,64]{1,0:T(8,128)S(1)}, f32[64,64]{0,1:T(8,128)S(1)}, s32[]{:T(128)}, s32[]{:T(128)}) while((s32[]{:T(128)}, f32[64,64]{1,0:T(8,128)S(1)}, f32[64,64]{0,1:T(8,128)S(1)}, s32[]{:T(128)}, s32[]{:T(128)}) %tuple.124), condition=%wide.region_3.4_spmd.clone.clone, body=%wide.region_2.3_spmd.clone.clone.sunk | while | flops 66051 | bytes 101992 | solution.py:32
  207.0 93.7 %while.55 = (s32[]{:T(128)}, f32[64,128]{1,0:T(8,128)S(1)}, f32[64,128]{1,0:T(8,128)S(1)}, f32[64,64]{1,0:T(8,128)S(1)}, s32[]{:T(128)}, /*index=5*/s32[]{:T(128)}, s32[]{:T(128)}) while((s32[]{:T(128)}, f32[64,128]{1,0:T(8,128)S(1)}, f32[64,128]{1,0:T(8,128)S(1)}, f32[64,64]{1,0:T(8,128)S(1)}, s32[]{:T(128)}, ...), condition=%wide.region_5.6_spmd.clone, body=%wide.region_4.5_spmd.clone.sunk | while | flops 131460 | bytes 102520 | solution.py:47
  207.6 0.8 fusion.76
  209.1 0.8 fusion.76
  210.5 0.8 fusion.76
  212.0 0.8 fusion.76
  213.5 0.8 fusion.76
  214.9 0.8 fusion.76
  216.4 0.8 fusion.76
  217.8 0.8 fusion.76
  219.3 0.8 fusion.76
  220.8 0.8 fusion.76
  222.2 0.8 fusion.76
  223.7 0.8 fusion.76
  225.2 0.8 fusion.76
  226.6 0.8 fusion.76
  228.1 0.8 fusion.76
  229.6 0.8 fusion.76
  231.0 0.8 fusion.76
  232.5 0.8 fusion.76
  234.0 0.8 fusion.76
  235.4 0.8 fusion.76
  236.9 0.8 fusion.76
  238.3 0.8 fusion.76
  239.8 0.8 fusion.76
  241.3 0.8 fusion.76
  242.7 0.8 fusion.76
  244.2 0.8 fusion.76
  245.7 0.8 fusion.76
  247.1 0.8 fusion.76
  248.6 0.8 fusion.76
  250.1 0.8 fusion.76
  251.5 0.8 fusion.76
  253.0 0.8 fusion.76
  254.5 0.8 fusion.76
  257.4 0.8 fusion.76
  276.4 0.8 fusion.76
  279.3 0.8 fusion.76
  282.3 0.8 fusion.76
  285.2 0.8 fusion.76
  301.3 23.1 %psum.22 = f32[64,64]{1,0:T(8,128)S(1)} all-reduce(f32[64,64]{1,0:T(8,128)S(1)} %fusion.53), channel_id=1, replica_groups=mesh['wide'=8,'blk'=4] {'wide'}, use_global_device_ids=true, to_apply=%region_6.7 | all-reduce | flops 4096 | bytes 32768 | tf_op jit(solution)/shard_map/psum | solution.py:10
  324.5 17.9 %psum.23 = f32[64,64]{1,0:T(8,128)S(1)} all-reduce(f32[64,64]{1,0:T(8,128)S(1)} %psum.22), channel_id=1, replica_groups=mesh['wide'=8,'blk'=4] {'blk'}, use_global_device_ids=true, to_apply=%region_7.8 | all-reduce | flops 4096 | bytes 32768 | tf_op jit(solution)/shard_map/psum | solution.py:11
  342.5 93.7 %while.56 = (s32[]{:T(128)}, f32[64,64]{1,0:T(8,128)S(1)}, f32[64,64]{1,0:T(8,128)S(1)}, f32[64,64]{1,0:T(8,128)S(1)}, s32[]{:T(128)}, /*index=5*/s32[]{:T(128)}, s32[]{:T(128)}, s32[]{:T(128)}) while((s32[]{:T(128)}, f32[64,64]{1,0:T(8,128)S(1)}, f32[64,64]{1,0:T(8,128)S(1)}, f32[64,64]{1,0:T(8,128)S(1)}, s32[]{:T(128)}, ...), condition=%wide.region_9.10_spmd.clone, body=%wide.region_8.9_spmd.clone.sunk | while | flops 65800 | bytes 69297 | solution.py:63
  346.0 0.8 fusion.79
  353.3 0.8 fusion.79
  360.7 0.8 fusion.79
  368.0 0.8 fusion.79
  373.8 0.8 fusion.79
  381.1 0.8 fusion.79
  388.5 0.8 fusion.79
  395.8 0.8 fusion.79
  401.6 0.8 fusion.79
  409.0 0.8 fusion.79
  416.3 0.8 fusion.79
  423.6 0.8 fusion.79
  429.4 0.8 fusion.79
  (881 shorter events, 208.8 us)
Async XLA Ops:
  7.2 37.4 %copy-start = (bf16[512,64]{0,1:T(8,128)(2,1)S(1)}, bf16[512,64]{0,1:T(8,128)(2,1)}, u32[]{:S(2)}) copy-start(bf16[512,64]{0,1:T(8,128)(2,1)} %param.19) | copy-start | bytes 196612
  7.2 60.7 %reduce-scatter.2.cloned.1.call-start = ((), (), s32[]{:S(2)}) async-start(), calls=%async_computation.1 | async-start | bytes 327680 | tf_op jit(solution)/shard_map/reduce_scatter | solution.py:154
  23.0 0.7 copy-start.6
  34.9 0.7 copy-start.7
  35.6 7.7 %copy-start.5 = (bf16[512]{0:T(512)(128)(2,1)S(1)}, bf16[512]{0:T(512)(128)(2,1)}, u32[]{:S(2)}) copy-start(bf16[512]{0:T(512)(128)(2,1)} %param.21) | copy-start | bytes 3076
  43.3 0.7 copy-start.4
  44.6 0.7 copy-start.8
  44.6 0.7 copy-start.9
  107.7 99.3 %copy-start.3 = (f32[128,128]{0,1:T(8,128)S(1)}, f32[128,128]{0,1:T(8,128)}, u32[]{:S(2)}) copy-start(f32[128,128]{0,1:T(8,128)} %reduce-scatter.2.cloned.1.call-done) | copy-start | bytes 196612
  300.7 0.6 copy-start.1
  436.2 0.6 copy-start.2
Sparse Core Ops, SparseCore 0:
  48.2 19.6 reduce-scatter.1
